TPU v7x, 32 devices: a whole 2x2x4 slice. The times are simulated.
32 devices in a mesh: grp: 4 (over y, x), fsdp: 8 (over z, core).
Axes of the slice: x: 2, y: 2, z: 4, core: 2. Of those that a mesh axis runs over, the one named last changes fastest.
Arguments:
- tokens: bfloat16 [64, 4096], P(('grp', 'fsdp')), may hold values from -128 to 128
- norm_gain: float32 [4096], replicated, may hold values from 0.25 to 1.75
- routes: int32 [64, 8], P(('grp', 'fsdp')), may hold values from 0 to 31, all different within a row; in each aligned block of 16 rows (0 to 15, 16 to 31, ...) at most 8 rows name the same one
- gate_probs: bfloat16 [64, 8], P(('grp', 'fsdp')), may hold values from 0.019897461 to 1
- w_gate_up: bfloat16 [32, 4096, 2048], P(('grp', 'fsdp')), may hold values from -0.09375 to 0.09375
- w_down: bfloat16 [32, 1024, 4096], P(('grp', 'fsdp')), may hold values from -0.1875 to 0.1875
Outputs:
- moe_out: bfloat16 [64, 4096], P(('grp', 'fsdp'))
Inputs may be any that keep to these rules, and one draw needn't show every extreme that they name: `routes`: each row names 8 different experts. In every aligned block of 16 rows no expert is named by more than 8 rows, a bound that some block reaches.
All inputs are finite; a program needn't handle non-finite values.
Results may differ from a plain program's by a relative error of at most 0.0095.
Values may be sent and summed in bfloat16 or wider, within the bound.
No kernel may reach another device: no remote copies, remote signals or barrier semaphores. Data moves between devices by JAX's collectives and lax.ppermute only.
A program may use at most 64 MiB of HBM per device.

v0:
```python
import jax
import jax.numpy as jnp
from jax import lax
from jax.sharding import PartitionSpec as P

FF = 1024


def local(tokens, norm_gain, routes, gate_probs, w_gate_up, w_down):
    group_count = lax.axis_size("grp")
    shard_count = lax.axis_size("fsdp")
    shard_index = lax.axis_index("fsdp")
    hidden_dev = w_down.shape[1]
    split_count = FF // hidden_dev
    expert_count = group_count * shard_count // split_count
    rows_dev = tokens.shape[0]
    top_count = routes.shape[1]
    block_rows = rows_dev * shard_count
    capacity = 2 * rows_dev * shard_count * top_count // expert_count
    width = tokens.shape[1]
    as_float = tokens.astype(jnp.float32)
    mean_square = jnp.mean(as_float * as_float, axis=-1, keepdims=True)
    normed = (as_float * lax.rsqrt(mean_square + 1e-06) * norm_gain).astype(jnp.bfloat16)
    rows_all, probs_all = (
        lax.all_gather(normed, "fsdp", axis=0, tiled=True),
        lax.all_gather(gate_probs, "fsdp", axis=0, tiled=True),
    )
    routes_all = lax.all_gather(routes, "fsdp", axis=0, tiled=True)
    probs = probs_all.astype(jnp.float32)
    combine = probs / jnp.sum(probs, axis=-1, keepdims=True)
    targets = (
        jnp.arange(group_count, dtype=jnp.int32) * (shard_count // split_count)
        + shard_index // split_count
    )
    matched = routes_all[None, :, :] == targets[:, None, None]
    is_routed = jnp.any(matched, axis=-1)
    row_weight = jnp.sum(jnp.where(matched, combine[None, :, :], 0.0), axis=-1)
    slot_index = jnp.cumsum(is_routed.astype(jnp.int32), axis=1) - 1
    select = (
        slot_index[:, None, :] == jnp.arange(capacity, dtype=jnp.int32)[None, :, None]
    ) & is_routed[:, None, :]
    outgoing = jnp.einsum(
        "gcb,bd->gcd", select.astype(jnp.bfloat16), rows_all, preferred_element_type=jnp.float32
    ).astype(jnp.bfloat16)
    incoming = lax.all_to_all(outgoing, "grp", split_axis=0, concat_axis=0, tiled=True)
    flattened = incoming.reshape(-1, width)
    projected = jnp.dot(flattened, w_gate_up[0], preferred_element_type=jnp.float32)
    hidden = (jax.nn.silu(projected[:, :hidden_dev]) * projected[:, hidden_dev:]).astype(
        jnp.bfloat16
    )
    result = jnp.dot(hidden, w_down[0], preferred_element_type=jnp.float32).astype(jnp.bfloat16)
    returned = lax.all_to_all(
        result.reshape(incoming.shape), "grp", split_axis=0, concat_axis=0, tiled=True
    )
    mix_matrix = (select.astype(jnp.float32) * row_weight[:, None, :]).reshape(-1, block_rows)
    row_partial = jnp.dot(
        mix_matrix.T,
        returned.reshape(-1, width),
        precision=lax.Precision.HIGHEST,
        preferred_element_type=jnp.float32,
    )
    summed = lax.psum_scatter(row_partial, "fsdp", scatter_dimension=0, tiled=True)
    return summed.astype(jnp.bfloat16)


def solution(mesh):
    return jax.shard_map(
        local,
        mesh=mesh,
        in_specs=(
            P(("grp", "fsdp"), None),
            P(),
            P(("grp", "fsdp"), None),
            P(("grp", "fsdp"), None),
            P(("grp", "fsdp"), None, None),
            P(("grp", "fsdp"), None, None),
        ),
        out_specs=P(("grp", "fsdp"), None),
        check_vma=False,
    )
```

profile of v0, /device:TPU:0, one launch (start us, length us, event | category | flops | bytes accessed | tf_op | source)
XLA Modules:
  0.0 94.8 jit_solution(7591240734302826050)
XLA Ops:
  0.0 0.9 fusion.14
  0.9 13.7 %all-gather = s32[8,2,8]{2,1,0:T(2,128)S(1)} all-gather(s32[1,2,8]{2,1,0:T(2,128)} %bitcast.29), channel_id=1, replica_groups=mesh['grp'=4,'fsdp'=8] {'fsdp'}, dimensions={0}, use_global_device_ids=true | all-gather | bytes 576 | tf_op jit(solution)/shard_map/all_gather | solution.py:28
  14.6 0.1 copy.7
  14.6 0.1 compare_reduce_fusion
  14.7 0.2 reduce_window_sum.11
  14.9 0.8 fusion.19
  15.7 14.0 %all-gather.2 = bf16[8,2,4096]{2,1,0:T(2,128)(2,1)S(1)} all-gather(bf16[1,2,4096]{2,1,0:T(2,128)(2,1)S(1)} %fusion.19), channel_id=1, replica_groups=mesh['grp'=4,'fsdp'=8] {'fsdp'}, dimensions={0}, use_global_device_ids=true | all-gather | bytes 147456 | tf_op jit(solution)/shard_map/all_gather | solution.py:25
  29.7 0.1 reshape.46
  29.8 0.9 convolution_convert_fusion
  30.7 3.7 %all-to-all-start = ((bf16[4,8,4096]{2,1,0:T(8,128)(2,1)}), bf16[4,8,4096]{2,1,0:T(8,128)(2,1)S(1)}, u32[]{:S(2)}, u32[]{:S(2)}) async-start(bf16[4,8,4096]{2,1,0:T(8,128)(2,1)} %convolution_convert_fusion), calls=%async_computation | async-start | bytes 524288 | tf_op jit(solution)/shard_map/all_to_all | solution.py:45
  34.4 8.8 %all-gather.1 = bf16[8,2,8]{2,1,0:T(2,128)(2,1)S(1)} all-gather(bf16[1,2,8]{2,1,0:T(2,128)(2,1)} %bitcast.30), channel_id=1, replica_groups=mesh['grp'=4,'fsdp'=8] {'fsdp'}, dimensions={0}, use_global_device_ids=true | all-gather | bytes 288 | tf_op jit(solution)/shard_map/all_gather | solution.py:26
  43.2 0.1 convert_reduce_fusion
  43.3 0.1 reshape.45
  43.4 0.0 copy-start.1
  43.4 0.0 all-to-all-done
  43.4 0.0 copy-start
  43.4 8.9 %fusion = f32[32,2048]{1,0:T(8,128)S(1)} fusion(bf16[1,4096,2048]{2,1,0:T(8,128)(2,1)} %param.10, bf16[4,8,4096]{2,1,0:T(8,128)(2,1)S(1)} %all-to-all-done), kind=kOutput, calls=%fused_computation | convolution fusion | flops 536870912 | bytes 17301504 | tf_op jit(solution)/shard_map/dot_general | solution.py:47
  52.3 0.0 copy-done
  52.3 2.2 %fusion.7 = bf16[4,8,4096]{2,1,0:T(8,128)(2,1)} fusion(bf16[1,1024,4096]{2,1,0:T(8,128)(2,1)S(1)} %copy-done, f32[32,2048]{1,0:T(8,128)S(1)} %fusion), kind=kOutput, calls=%fused_computation.6 | convolution fusion | flops 268763136 | bytes 8912896 | tf_op jit(solution)/shard_map/dot_general | solution.py:51
  54.5 4.2 %all-to-all-start.1 = ((bf16[4,8,4096]{2,1,0:T(8,128)(2,1)}), bf16[4,8,4096]{2,1,0:T(8,128)(2,1)S(1)}, u32[]{:S(2)}, u32[]{:S(2)}) async-start(bf16[4,8,4096]{2,1,0:T(8,128)(2,1)} %fusion.7), calls=%async_computation.1 | async-start | bytes 524288 | tf_op jit(solution)/shard_map/all_to_all | solution.py:52
  58.7 0.1 broadcast_divide_fusion
  58.8 0.1 copy.8
  58.9 0.0 copy-done.1
  58.9 0.6 dynamic-slice
  60.1 0.1 fusion.17
  60.2 4.4 %all-to-all-done.1 = bf16[4,8,4096]{2,1,0:T(8,128)(2,1)S(1)} async-done(((bf16[4,8,4096]{2,1,0:T(8,128)(2,1)}), bf16[4,8,4096]{2,1,0:T(8,128)(2,1)S(1)}, u32[]{:S(2)}, u32[]{:S(2)}) %all-to-all-start.1) | async-done | bytes 262176 | tf_op jit(solution)/shard_map/all_to_all | solution.py:52
  64.6 0.3 convolution_bitcast_fusion
  64.9 29.2 %all-reduce.2 = bf16[16,4096]{1,0:T(8,128)(2,1)S(1)} all-reduce(f32[16,4096]{1,0:T(8,128)S(1)} %convolution_bitcast_fusion), channel_id=2, replica_groups=mesh['grp'=4,'fsdp'=8] {'fsdp'}, use_global_device_ids=true, to_apply=%region_5.6.clone | all-reduce | flops 65536 | bytes 393216
  94.1 0.6 dynamic-slice_convert_fusion
  (4 shorter events, 0.0 us)
Async XLA Ops:
  30.7 12.7 %all-to-all-start = ((bf16[4,8,4096]{2,1,0:T(8,128)(2,1)}), bf16[4,8,4096]{2,1,0:T(8,128)(2,1)S(1)}, u32[]{:S(2)}, u32[]{:S(2)}) async-start(bf16[4,8,4096]{2,1,0:T(8,128)(2,1)} %convolution_convert_fusion), calls=%async_computation | async-start | bytes 524288 | tf_op jit(solution)/shard_map/all_to_all | solution.py:45
  43.4 15.5 %copy-start.1 = (u32[32]{0:T(128)S(1)}, u32[32]{0:T(128)}, u32[]{:S(2)}) copy-start(u32[32]{0:T(128)} %constant.44) | copy-start | bytes 388
  43.4 8.9 %copy-start = (bf16[1,1024,4096]{2,1,0:T(8,128)(2,1)S(1)}, bf16[1,1024,4096]{2,1,0:T(8,128)(2,1)}, u32[]{:S(2)}) copy-start(bf16[1,1024,4096]{2,1,0:T(8,128)(2,1)} %param.11) | copy-start | bytes 25165828
  54.5 10.0 %all-to-all-start.1 = ((bf16[4,8,4096]{2,1,0:T(8,128)(2,1)}), bf16[4,8,4096]{2,1,0:T(8,128)(2,1)S(1)}, u32[]{:S(2)}, u32[]{:S(2)}) async-start(bf16[4,8,4096]{2,1,0:T(8,128)(2,1)} %fusion.7), calls=%async_computation.1 | async-start | bytes 524288 | tf_op jit(solution)/shard_map/all_to_all | solution.py:52
where the time goes:
time: 95.3 us; the launch traced here: 94.8 us
  blocking collectives  65.7 us (69%)
  matrix products  12.4 us (13%)
  starting transfers between devices  7.91 us (8%)
  waiting for transfers between devices  4.35 us (5%)
  other arithmetic  2.24 us (2%)
  local copies, waits for them, and re-layouts  1.5 us (2%)
    unnamed x1, blocking collectives  29.2 us
    all_gather x1, blocking collectives, local(): lax.all_gather(normed, 'fsdp', axis=0, tiled=True)  14 us
    all_gather x1, blocking collectives, local(): routes_all = lax.all_gather(routes, 'fsdp', axis=0, tiled=True)  13.7 us
    dot_general x1, matrix products, local(): jnp.dot(flattened, w_gate_up[0], preferred_element_type=jnp.float32)  8.9 us
    all_gather x1, blocking collectives, local(): lax.all_gather(gate_probs, 'fsdp', axis=0, tiled=True)  8.82 us
    all_to_all x1, waiting for transfers between devices, local(): lax.all_to_all(result.reshape(incoming.shape), 'grp', split_axis=0, conca...  4.35 us
    all_to_all x1, starting transfers between devices, local(): lax.all_to_all(result.reshape(incoming.shape), 'grp', split_axis=0, conca...  4.19 us
    all_to_all x1, starting transfers between devices, local(): lax.all_to_all(outgoing, 'grp', split_axis=0, concat_axis=0, tiled=True)  3.71 us
  transfers between devices with their start and end apart: 2, of which 1 were waited for; matrix products, arithmetic and copies ran while one was open for 1% of the time, Pallas kernels for 0%

commit v1 on v0

--- a/solution.py
+++ b/solution.py
@@ -4,6 +4,21 @@
 from jax.sharding import PartitionSpec as P
 
 FF = 1024
+
+
+def process_the_tables(base_x):
+    ax_name = "fsdp"
+    k_all = lax.axis_size(ax_name)
+    copies = tuple(((kk, (kk + 1) % k_all) for kk in range(k_all)))
+    all_blocks = tuple(((kk, (kk - 1) % k_all) for kk in range(k_all)))
+    built, before = ([base_x], [base_x])
+    for _ in range(k_all // 2):
+        z = lax.ppermute(built[-1], ax_name, copies)
+        built.append(z)
+    for _ in range((k_all - 1) // 2):
+        before.append(lax.ppermute(before[-1], ax_name, all_blocks))
+    y = jnp.concatenate([*built[::-1], *before[1:]], axis=0)
+    return jnp.roll(y, (lax.axis_index(ax_name) - k_all // 2) * base_x.shape[0], axis=0)
 
 
 def local(tokens, norm_gain, routes, gate_probs, w_gate_up, w_down):
@@ -23,7 +38,7 @@
     normed = (as_float * lax.rsqrt(mean_square + 1e-06) * norm_gain).astype(jnp.bfloat16)
     rows_all, probs_all = (
         lax.all_gather(normed, "fsdp", axis=0, tiled=True),
-        lax.all_gather(gate_probs, "fsdp", axis=0, tiled=True),
+        process_the_tables(gate_probs),
     )
     routes_all = lax.all_gather(routes, "fsdp", axis=0, tiled=True)
     probs = probs_all.astype(jnp.float32)

time: 95.3 us -> 106 us (1.11)
  starting transfers between devices: 7.91 us -> 18.5 us
  blocking collectives: 65.7 us -> 56.6 us
  waiting for transfers between devices: 4.35 us -> 12.6 us
  local copies, waits for them, and re-layouts: 1.5 us -> 2.84 us
    ppermute x0 -> x7, starting transfers between devices: none -> 10.6 us  [the longest x3 10.5 us: process_the_tables(): before.append(lax.ppermute(before[-1], ax_name, all_blocks))]
    all_gather x1 -> x0, blocking collectives: 8.82 us -> none  [local(): lax.all_gather(gate_probs, 'fsdp', axis=0, tiled=True)]
    ppermute x0 -> x7, waiting for transfers between devices: none -> 7.38 us  [the longest x4 7.28 us: process_the_tables(): z = lax.ppermute(built[-1], ax_name, copies)]
    unnamed x7 -> x6, local copies, waits for them, and re-layouts: 0.72 us -> 2.1 us
  transfers between devices with their start and end apart: 2 -> 9, of which waited for: 1 -> 4; matrix products, arithmetic and copies ran while one was open for 1% -> 2% of each run, Pallas kernels for 0% -> 0%
where the time goes in v1:
time: 106 us
  blocking collectives  56.6 us (53%)
  starting transfers between devices  18.5 us (17%)
  waiting for transfers between devices  12.6 us (12%)
  matrix products  12.4 us (12%)
  local copies, waits for them, and re-layouts  2.84 us (3%)
  other arithmetic  2.25 us (2%)
    unnamed x1, blocking collectives  29 us
    all_gather x1, blocking collectives, local(): lax.all_gather(normed, 'fsdp', axis=0, tiled=True)  14 us
    all_gather x1, blocking collectives, local(): routes_all = lax.all_gather(routes, 'fsdp', axis=0, tiled=True)  13.7 us
    ppermute x3, starting transfers between devices, process_the_tables(): before.append(lax.ppermute(before[-1], ax_name, all_blocks))  10.5 us
    dot_general x1, matrix products, local(): jnp.dot(flattened, w_gate_up[0], preferred_element_type=jnp.float32)  8.9 us
    ppermute x4, waiting for transfers between devices, process_the_tables(): z = lax.ppermute(built[-1], ax_name, copies)  7.28 us
    all_to_all x1, waiting for transfers between devices, local(): lax.all_to_all(result.reshape(incoming.shape), 'grp', split_axis=0, conca...  5.21 us
    all_to_all x1, starting transfers between devices, local(): lax.all_to_all(result.reshape(incoming.shape), 'grp', split_axis=0, conca...  4.19 us
  transfers between devices with their start and end apart: 9, of which 4 were waited for; matrix products, arithmetic and copies ran while one was open for 2% of the time, Pallas kernels for 0%

profile of v1, /device:TPU:0, one launch (start us, length us, event | category | flops | bytes accessed | tf_op | source)
XLA Modules:
  0.0 105.9 jit_solution(17942365301292912977)
XLA Ops:
  0.0 13.7 %all-gather = s32[8,2,8]{2,1,0:T(2,128)S(1)} all-gather(s32[1,2,8]{2,1,0:T(2,128)} %bitcast.25), channel_id=1, replica_groups=mesh['grp'=4,'fsdp'=8] {'fsdp'}, dimensions={0}, use_global_device_ids=true | all-gather | bytes 576 | tf_op jit(solution)/shard_map/all_gather | solution.py:43
  13.7 0.1 copy.12
  13.7 0.1 compare_reduce_fusion
  13.8 0.2 reduce_window_sum.11
  14.0 0.9 fusion.14
  14.9 0.8 fusion.19
  15.7 14.0 %all-gather.1 = bf16[8,2,4096]{2,1,0:T(2,128)(2,1)S(1)} all-gather(bf16[1,2,4096]{2,1,0:T(2,128)(2,1)S(1)} %fusion.19), channel_id=1, replica_groups=mesh['grp'=4,'fsdp'=8] {'fsdp'}, dimensions={0}, use_global_device_ids=true | all-gather | bytes 147456 | tf_op jit(solution)/shard_map/all_gather | solution.py:40
  29.7 0.1 reshape.42
  29.8 0.9 convolution_convert_fusion
  30.7 3.7 %all-to-all-start = ((bf16[4,8,4096]{2,1,0:T(8,128)(2,1)}), bf16[4,8,4096]{2,1,0:T(8,128)(2,1)S(1)}, u32[]{:S(2)}, u32[]{:S(2)}) async-start(bf16[4,8,4096]{2,1,0:T(8,128)(2,1)} %convolution_convert_fusion), calls=%async_computation | async-start | bytes 524288 | tf_op jit(solution)/shard_map/all_to_all | solution.py:60
  34.4 0.7 copy.13
  35.1 0.1 collective-permute-start
  35.2 3.5 %collective-permute-start.4 = (bf16[2,8]{0,1:T(8,128)(2,1)S(1)}, bf16[2,8]{0,1:T(8,128)(2,1)S(1)}, u32[]{:S(2)}, u32[]{:S(2)}) collective-permute-start(bf16[2,8]{0,1:T(8,128)(2,1)S(1)} %copy.13), channel_id=1, source_target_pairs={{0,7},{1,0},{2,1},{3,2},{4,3},{5,4},{6,5},{7,6},{8,15},{9,8},{10,9... | collective-permute-start | bytes 104 | tf_op jit(solution)/shard_map/ppermute | solution.py:19
  38.7 1.2 %dynamic-slice = u32[1]{0:T(128)} dynamic-slice(u32[32]{0:T(128)} %constant.70, u32[]{:T(128)S(6)} %add.48), dynamic_slice_sizes={1} | dynamic-slice | bytes 12
  40.6 0.1 collective-permute-start.1
  40.6 3.5 %collective-permute-start.5 = (bf16[2,8]{0,1:T(8,128)(2,1)S(1)}, bf16[2,8]{0,1:T(8,128)(2,1)S(1)}, u32[]{:S(2)}, u32[]{:S(2)}) collective-permute-start(bf16[2,8]{0,1:T(8,128)(2,1)S(1)} %collective-permute-done.4), channel_id=1, source_target_pairs={{0,7},{1,0},{2,1},{3,2},{4,3},{5,4},{6,5},{7,6},{8,15},{9,8},{10,9... | collective-permute-start | bytes 104 | tf_op jit(solution)/shard_map/ppermute | solution.py:19
  44.2 1.3 %collective-permute-done.1 = bf16[2,8]{0,1:T(8,128)(2,1)S(1)} collective-permute-done((bf16[2,8]{0,1:T(8,128)(2,1)S(1)}, bf16[2,8]{0,1:T(8,128)(2,1)S(1)}, u32[]{:S(2)}, u32[]{:S(2)}) %collective-permute-start.1) | collective-permute-done | bytes 64 | tf_op jit(solution)/shard_map/ppermute | solution.py:16
  45.4 0.0 collective-permute-done.5
  45.5 3.5 %collective-permute-start.6 = (bf16[2,8]{0,1:T(8,128)(2,1)S(1)}, bf16[2,8]{0,1:T(8,128)(2,1)S(1)}, u32[]{:S(2)}, u32[]{:S(2)}) collective-permute-start(bf16[2,8]{0,1:T(8,128)(2,1)S(1)} %collective-permute-done.5), channel_id=1, source_target_pairs={{0,7},{1,0},{2,1},{3,2},{4,3},{5,4},{6,5},{7,6},{8,15},{9,8},{10,9... | collective-permute-start | bytes 104 | tf_op jit(solution)/shard_map/ppermute | solution.py:19
  49.0 1.3 %collective-permute-done.2 = bf16[2,8]{0,1:T(8,128)(2,1)S(1)} collective-permute-done((bf16[2,8]{0,1:T(8,128)(2,1)S(1)}, bf16[2,8]{0,1:T(8,128)(2,1)S(1)}, u32[]{:S(2)}, u32[]{:S(2)}) %collective-permute-start.2) | collective-permute-done | bytes 64 | tf_op jit(solution)/shard_map/ppermute | solution.py:16
  50.3 4.8 %collective-permute-done.3 = bf16[2,8]{0,1:T(8,128)(2,1)S(1)} collective-permute-done((bf16[2,8]{0,1:T(8,128)(2,1)S(1)}, bf16[2,8]{0,1:T(8,128)(2,1)S(1)}, u32[]{:S(2)}, u32[]{:S(2)}) %collective-permute-start.3) | collective-permute-done | bytes 64 | tf_op jit(solution)/shard_map/ppermute | solution.py:16
  55.0 0.1 concatenate.6
  55.1 0.1 convert_reduce_fusion
  55.2 8.9 %fusion = f32[32,2048]{1,0:T(8,128)S(1)} fusion(bf16[1,4096,2048]{2,1,0:T(8,128)(2,1)} %param.10, bf16[4,8,4096]{2,1,0:T(8,128)(2,1)S(1)} %all-to-all-done), kind=kOutput, calls=%fused_computation | convolution fusion | flops 536870912 | bytes 17301504 | tf_op jit(solution)/shard_map/dot_general | solution.py:62
  64.1 2.2 %fusion.7 = bf16[4,8,4096]{2,1,0:T(8,128)(2,1)} fusion(bf16[1,1024,4096]{2,1,0:T(8,128)(2,1)S(1)} %copy-done, f32[32,2048]{1,0:T(8,128)S(1)} %fusion), kind=kOutput, calls=%fused_computation.6 | convolution fusion | flops 268763136 | bytes 8912896 | tf_op jit(solution)/shard_map/dot_general | solution.py:66
  66.4 4.2 %all-to-all-start.1 = ((bf16[4,8,4096]{2,1,0:T(8,128)(2,1)}), bf16[4,8,4096]{2,1,0:T(8,128)(2,1)S(1)}, u32[]{:S(2)}, u32[]{:S(2)}) async-start(bf16[4,8,4096]{2,1,0:T(8,128)(2,1)} %fusion.7), calls=%async_computation.1 | async-start | bytes 524288 | tf_op jit(solution)/shard_map/all_to_all | solution.py:67
  70.6 0.1 convert_divide_fusion
  70.6 0.1 fusion.17
  70.7 5.2 %all-to-all-done.1 = bf16[4,8,4096]{2,1,0:T(8,128)(2,1)S(1)} async-done(((bf16[4,8,4096]{2,1,0:T(8,128)(2,1)}), bf16[4,8,4096]{2,1,0:T(8,128)(2,1)S(1)}, u32[]{:S(2)}, u32[]{:S(2)}) %all-to-all-start.1) | async-done | bytes 262176 | tf_op jit(solution)/shard_map/all_to_all | solution.py:67
  75.9 0.3 convolution_bitcast_fusion
  76.3 29.0 %all-reduce.2 = bf16[16,4096]{1,0:T(8,128)(2,1)S(1)} all-reduce(f32[16,4096]{1,0:T(8,128)S(1)} %convolution_bitcast_fusion), channel_id=2, replica_groups=mesh['grp'=4,'fsdp'=8] {'fsdp'}, use_global_device_ids=true, to_apply=%region_5.6.clone | all-reduce | flops 65536 | bytes 393216
  105.2 0.6 dynamic-slice_convert_fusion
  (12 shorter events, 0.1 us)
Async XLA Ops:
  30.7 24.6 %all-to-all-start = ((bf16[4,8,4096]{2,1,0:T(8,128)(2,1)}), bf16[4,8,4096]{2,1,0:T(8,128)(2,1)S(1)}, u32[]{:S(2)}, u32[]{:S(2)}) async-start(bf16[4,8,4096]{2,1,0:T(8,128)(2,1)} %convolution_convert_fusion), calls=%async_computation | async-start | bytes 524288 | tf_op jit(solution)/shard_map/all_to_all | solution.py:60
  35.1 5.4 %collective-permute-start = (bf16[2,8]{0,1:T(8,128)(2,1)S(1)}, bf16[2,8]{0,1:T(8,128)(2,1)S(1)}, u32[]{:S(2)}, u32[]{:S(2)}) collective-permute-start(bf16[2,8]{0,1:T(8,128)(2,1)S(1)} %copy.13), channel_id=1, source_target_pairs={{0,1},{1,2},{2,3},{3,4},{4,5},{5,6},{6,7},{7,0},{8,9},{9,10},{10,1... | collective-permute-start | bytes 104 | tf_op jit(solution)/shard_map/ppermute | solution.py:16
  35.2 5.5 %collective-permute-start.4 = (bf16[2,8]{0,1:T(8,128)(2,1)S(1)}, bf16[2,8]{0,1:T(8,128)(2,1)S(1)}, u32[]{:S(2)}, u32[]{:S(2)}) collective-permute-start(bf16[2,8]{0,1:T(8,128)(2,1)S(1)} %copy.13), channel_id=1, source_target_pairs={{0,7},{1,0},{2,1},{3,2},{4,3},{5,4},{6,5},{7,6},{8,15},{9,8},{10,9... | collective-permute-start | bytes 104 | tf_op jit(solution)/shard_map/ppermute | solution.py:19
  40.6 4.9 %collective-permute-start.1 = (bf16[2,8]{0,1:T(8,128)(2,1)S(1)}, bf16[2,8]{0,1:T(8,128)(2,1)S(1)}, u32[]{:S(2)}, u32[]{:S(2)}) collective-permute-start(bf16[2,8]{0,1:T(8,128)(2,1)S(1)} %collective-permute-done), channel_id=1, source_target_pairs={{0,1},{1,2},{2,3},{3,4},{4,5},{5,6},{6,7},{7,0},{8,9},{9,10},{10,1... | collective-permute-start | bytes 104 | tf_op jit(solution)/shard_map/ppermute | solution.py:16
  40.6 4.8 %collective-permute-start.5 = (bf16[2,8]{0,1:T(8,128)(2,1)S(1)}, bf16[2,8]{0,1:T(8,128)(2,1)S(1)}, u32[]{:S(2)}, u32[]{:S(2)}) collective-permute-start(bf16[2,8]{0,1:T(8,128)(2,1)S(1)} %collective-permute-done.4), channel_id=1, source_target_pairs={{0,7},{1,0},{2,1},{3,2},{4,3},{5,4},{6,5},{7,6},{8,15},{9,8},{10,9... | collective-permute-start | bytes 104 | tf_op jit(solution)/shard_map/ppermute | solution.py:19
  45.4 4.8 %collective-permute-start.2 = (bf16[2,8]{0,1:T(8,128)(2,1)S(1)}, bf16[2,8]{0,1:T(8,128)(2,1)S(1)}, u32[]{:S(2)}, u32[]{:S(2)}) collective-permute-start(bf16[2,8]{0,1:T(8,128)(2,1)S(1)} %collective-permute-done.1), channel_id=1, source_target_pairs={{0,1},{1,2},{2,3},{3,4},{4,5},{5,6},{6,7},{7,0},{8,9},{9,10},{10,1... | collective-permute-start | bytes 104 | tf_op jit(solution)/shard_map/ppermute | solution.py:16
  45.5 4.8 %collective-permute-start.6 = (bf16[2,8]{0,1:T(8,128)(2,1)S(1)}, bf16[2,8]{0,1:T(8,128)(2,1)S(1)}, u32[]{:S(2)}, u32[]{:S(2)}) collective-permute-start(bf16[2,8]{0,1:T(8,128)(2,1)S(1)} %collective-permute-done.5), channel_id=1, source_target_pairs={{0,7},{1,0},{2,1},{3,2},{4,3},{5,4},{6,5},{7,6},{8,15},{9,8},{10,9... | collective-permute-start | bytes 104 | tf_op jit(solution)/shard_map/ppermute | solution.py:19
  50.2 4.8 %collective-permute-start.3 = (bf16[2,8]{0,1:T(8,128)(2,1)S(1)}, bf16[2,8]{0,1:T(8,128)(2,1)S(1)}, u32[]{:S(2)}, u32[]{:S(2)}) collective-permute-start(bf16[2,8]{0,1:T(8,128)(2,1)S(1)} %collective-permute-done.2), channel_id=1, source_target_pairs={{0,1},{1,2},{2,3},{3,4},{4,5},{5,6},{6,7},{7,0},{8,9},{9,10},{10,1... | collective-permute-start | bytes 104 | tf_op jit(solution)/shard_map/ppermute | solution.py:16
  55.2 8.9 %copy-start = (bf16[1,1024,4096]{2,1,0:T(8,128)(2,1)S(1)}, bf16[1,1024,4096]{2,1,0:T(8,128)(2,1)}, u32[]{:S(2)}) copy-start(bf16[1,1024,4096]{2,1,0:T(8,128)(2,1)} %param.11) | copy-start | bytes 25165828
  66.4 9.6 %all-to-all-start.1 = ((bf16[4,8,4096]{2,1,0:T(8,128)(2,1)}), bf16[4,8,4096]{2,1,0:T(8,128)(2,1)S(1)}, u32[]{:S(2)}, u32[]{:S(2)}) async-start(bf16[4,8,4096]{2,1,0:T(8,128)(2,1)} %fusion.7), calls=%async_computation.1 | async-start | bytes 524288 | tf_op jit(solution)/shard_map/all_to_all | solution.py:67
